TPU v7x, 32 devices: a whole 2x2x4 slice. The times are simulated.
32 devices in a mesh: lat: 4 (over y, x), lon: 8 (over z, core).
Axes of the slice: x: 2, y: 2, z: 4, core: 2. Of those that a mesh axis runs over, the one named last changes fastest.
Arguments:
- right_side: float32 [512, 2048], P('lat', 'lon'), may hold values from -12 to 12
- diagonal: float32 [512, 2048], P('lat', 'lon'), may hold values from 0.2 to 2
- east_coef: float32 [512, 2048], P('lat', 'lon'), may hold values from 0.5 to 2
- north_coef: float32 [512, 2048], P('lat', 'lon'), may hold values from 0.5 to 2
- land_sea: int32 [512, 2048], P('lat', 'lon'), may hold values 0 or 1
- fold_partner: int32 [2048], P('lon'), may hold values from 0 to 2047, as said below
Outputs:
- solution_field: float32 [512, 2048], P('lat', 'lon')
- residual: float32 [512, 2048], P('lat', 'lon')
Inputs may be any that keep to these rules, and one draw needn't show every extreme that they name: fold_partner[fold_partner[i]] = i and fold_partner[i] != i for every column i, and fold_partner[i] // 256 = 7 - i // 256.
All inputs are finite; a program needn't handle non-finite values. No bound on the sum of `land_sea` on one device may be relied on, other than what follows from the above.
Results may differ from a plain program's by a relative error of at most 0.00019.
Values sent between devices are 32-bit elements; how exact they have to be, the bound alone decides.
A program may use at most 64 MiB of HBM per device.

v0:
```python
import jax
import jax.numpy as jnp
from jax import lax
from jax.sharding import PartitionSpec as P

ITERS = 4


def with_halo(cells, sides, width, closed):
    for axis, dim in sides:
        count = lax.axis_size(axis)
        ends = count if closed else count - 1
        head = lax.slice_in_dim(cells, 0, width, axis=dim)
        tail = lax.slice_in_dim(cells, cells.shape[dim] - width, cells.shape[dim], axis=dim)
        cells = jnp.concatenate(
            [
                lax.ppermute(tail, axis, [(i, (i + 1) % count) for i in range(ends)]),
                cells,
                lax.ppermute(head, axis, [((i + 1) % count, i) for i in range(ends)]),
            ],
            axis=dim,
        )
    return cells


def zonal_rim(values):
    return with_halo(values, (("lon", 1),), 1, True)


def meridional_rim(values):
    return with_halo(values, (("lat", 0),), 1, False)


def paired(residual, image):
    return lax.psum((jnp.sum(residual * residual), jnp.sum(residual * image)), ("lat", "lon"))


def local(right_side, diagonal, east_coef, north_coef, land_sea, fold_partner):
    row_count, col_count = right_side.shape
    ocean = land_sea.astype(jnp.float32)
    on_top = lax.axis_index("lat") == lax.axis_size("lat") - 1
    row_ids = lax.broadcasted_iota(jnp.int32, (row_count, col_count), 0)
    north_inner = jnp.where(on_top & (row_ids == row_count - 1), 0.0, north_coef)
    west_coef = zonal_rim(east_coef)[:, :col_count]
    south_coef = meridional_rim(north_inner)[:row_count]

    def neighbours(masked):
        across_lon = zonal_rim(masked)
        across_lat = meridional_rim(masked)
        return (
            across_lon[:, 2:],
            across_lon[:, :col_count],
            across_lat[2:],
            across_lat[:row_count],
        )

    def mirror_row(top_values):
        whole_row = lax.all_gather(top_values, "lon", axis=0, tiled=True)
        return jnp.take(whole_row, fold_partner, axis=0)

    top_coef = north_coef[row_count - 1]
    fold_coef = jnp.where(on_top, 0.5 * (top_coef + mirror_row(top_coef)), 0.0)

    def operate(surface):
        masked = ocean * surface
        east_vals, west_vals, north_vals, south_vals = neighbours(masked)
        spread = east_coef * (masked - east_vals) + west_coef * (masked - west_vals)
        spread = spread + north_inner * (masked - north_vals) + south_coef * (masked - south_vals)
        last_row = masked[row_count - 1]
        spread = spread.at[row_count - 1].add(fold_coef * (last_row - mirror_row(last_row)))
        return diagonal * surface + ocean * spread

    solution_field = jnp.zeros_like(right_side)
    residual = right_side
    image = operate(residual)
    norm_now, product = paired(residual, image)
    alpha = norm_now / product
    direction, along = (residual, image)
    for iteration in range(ITERS):
        solution_field = solution_field + alpha * direction
        residual = residual - alpha * along
        if iteration + 1 < ITERS:
            image = operate(residual)
            norm_next, product = paired(residual, image)
            ratio = norm_next / norm_now
            alpha = norm_next / (product - ratio * norm_next / alpha)
            direction = residual + ratio * direction
            along = image + ratio * along
            norm_now = norm_next
    return (solution_field, residual)


def solution(mesh):
    placed = (
        P("lat", "lon"),
        P("lat", "lon"),
        P("lat", "lon"),
        P("lat", "lon"),
        P("lat", "lon"),
        P("lon"),
    )
    return jax.shard_map(
        local,
        mesh=mesh,
        in_specs=placed,
        out_specs=(P("lat", "lon"), P("lat", "lon")),
        check_vma=False,
    )
```

profile of v0, /device:TPU:0, one launch (start us, length us, event | category | flops | bytes accessed | tf_op | source)
XLA Modules:
  0.0 291.4 jit_solution(6611212178361798222)
XLA Ops:
  0.6 1.0 slice.203
  1.6 0.5 collective-permute-start.1
  2.2 0.1 broadcast_select_fusion
  2.3 4.4 %collective-permute-start.4 = (f32[1,256]{1,0:T(1,128)S(1)}, f32[1,256]{1,0:T(1,128)S(1)}, u32[]{:S(2)}, u32[]{:S(2)}) collective-permute-start(f32[1,256]{1,0:T(1,128)S(1)} %slice.255), channel_id=1, source_target_pairs={{0,8},{8,16},{16,24},{1,9},{9,17},{17,25},{2,10},{10,18},{18,26},{... | collective-permute-start | bytes 3080 | tf_op jit(solution)/shard_map/ppermute | solution.py:17
  6.7 1.3 collective-permute-start.3
  8.0 4.5 %collective-permute-start.5 = (f32[1,256]{1,0:T(1,128)S(1)}, f32[1,256]{1,0:T(1,128)S(1)}, u32[]{:S(2)}, u32[]{:S(2)}) collective-permute-start(f32[1,256]{1,0:T(1,128)S(1)} %get-tuple-element.88), channel_id=1, source_target_pairs={{0,8},{8,16},{16,24},{1,9},{9,17},{17,25},{2,10},{10,18},{18,26},{... | collective-permute-start | bytes 3080 | tf_op jit(solution)/shard_map/ppermute | solution.py:17
  12.7 2.7 collective-permute-start
  15.4 10.3 %all-gather.1 = f32[1,2048]{1,0:T(1,128)S(1)} all-gather(f32[1,256]{1,0:T(1,128)S(1)} %get-tuple-element.88), channel_id=3, replica_groups=mesh['lat'=4,'lon'=8] {'lon'}, dimensions={1}, use_global_device_ids=true | all-gather | bytes 9216 | tf_op jit(solution)/shard_map/all_gather | solution.py:58
  25.7 8.8 %all-gather = f32[1,2048]{1,0:T(1,128)S(1)} all-gather(f32[1,256]{1,0:T(1,128)S(1)} %slice.214), channel_id=2, replica_groups=mesh['lat'=4,'lon'=8] {'lon'}, dimensions={1}, use_global_device_ids=true | all-gather | bytes 9216 | tf_op jit(solution)/shard_map/all_gather | solution.py:58
  34.5 1.7 gather_fusion
  36.2 1.7 gather_fusion.1
  37.9 0.4 collective-permute-start.2
  38.4 5.1 %collective-permute-done.2 = f32[128,1]{1,0:T(8,128)S(1)} collective-permute-done((f32[128,1]{1,0:T(8,128)S(1)}, f32[128,1]{1,0:T(8,128)S(1)}, u32[]{:S(2)}, u32[]{:S(2)}) %collective-permute-start.2) | collective-permute-done | bytes 544 | tf_op jit(solution)/shard_map/ppermute | solution.py:17
  43.5 0.2 fusion.35
  43.8 0.7 multiply_reduce_fusion.6
  44.4 38.3 %all-reduce.3 = (f32[]{:T(128)}, f32[]{:T(128)}) all-reduce(f32[]{:T(128)} %get-tuple-element.58, f32[]{:T(128)} %get-tuple-element.57), channel_id=1, replica_groups=mesh['lat'=4,'lon'=8] {'lat','lon'}, use_global_device_ids=true, to_apply=%region_1.2 | all-reduce | flops 2 | bytes 16 | tf_op jit(solution)/shard_map/psum | solution.py:35
  84.1 10.5 %all-gather.2 = f32[1,2048]{1,0:T(1,128)S(1)} all-gather(f32[1,256]{1,0:T(1,128)S(1)} %get-tuple-element.84), channel_id=4, replica_groups=mesh['lat'=4,'lon'=8] {'lon'}, dimensions={1}, use_global_device_ids=true | all-gather | bytes 9216 | tf_op jit(solution)/shard_map/all_gather | solution.py:58
  94.6 4.2 %collective-permute-start.9 = (f32[1,256]{1,0:T(1,128)S(1)}, f32[1,256]{1,0:T(1,128)S(1)}, u32[]{:S(2)}, u32[]{:S(2)}) collective-permute-start(f32[1,256]{1,0:T(1,128)S(1)} %get-tuple-element.84), channel_id=1, source_target_pairs={{0,8},{8,16},{16,24},{1,9},{9,17},{17,25},{2,10},{10,18},{18,26},{... | collective-permute-start | bytes 3080 | tf_op jit(solution)/shard_map/ppermute | solution.py:17
  98.8 1.7 gather_fusion.2
  100.6 1.3 collective-permute-start.8
  101.9 0.5 collective-permute-start.7
  102.4 1.4 collective-permute-done.6
  103.8 3.6 %collective-permute-done.7 = f32[128,1]{1,0:T(8,128)S(1)} collective-permute-done((f32[128,1]{1,0:T(8,128)S(1)}, f32[128,1]{1,0:T(8,128)S(1)}, u32[]{:S(2)}, u32[]{:S(2)}) %collective-permute-start.7) | collective-permute-done | bytes 544 | tf_op jit(solution)/shard_map/ppermute | solution.py:17
  107.5 0.2 fusion.24
  107.8 0.7 multiply_reduce_fusion.4
  108.5 40.3 %all-reduce.2 = (f32[]{:T(128)}, f32[]{:T(128)}) all-reduce(f32[]{:T(128)} %get-tuple-element.54, f32[]{:T(128)} %get-tuple-element.53), channel_id=1, replica_groups=mesh['lat'=4,'lon'=8] {'lat','lon'}, use_global_device_ids=true, to_apply=%region_5.7 | all-reduce | flops 2 | bytes 16 | tf_op jit(solution)/shard_map/psum | solution.py:35
  153.4 10.9 %all-gather.3 = f32[1,2048]{1,0:T(1,128)S(1)} all-gather(f32[1,256]{1,0:T(1,128)S(1)} %get-tuple-element.80), channel_id=5, replica_groups=mesh['lat'=4,'lon'=8] {'lon'}, dimensions={1}, use_global_device_ids=true | all-gather | bytes 9216 | tf_op jit(solution)/shard_map/all_gather | solution.py:58
  164.3 4.2 %collective-permute-start.13 = (f32[1,256]{1,0:T(1,128)S(1)}, f32[1,256]{1,0:T(1,128)S(1)}, u32[]{:S(2)}, u32[]{:S(2)}) collective-permute-start(f32[1,256]{1,0:T(1,128)S(1)} %get-tuple-element.80), channel_id=1, source_target_pairs={{0,8},{8,16},{16,24},{1,9},{9,17},{17,25},{2,10},{10,18},{18,26},{... | collective-permute-start | bytes 3080 | tf_op jit(solution)/shard_map/ppermute | solution.py:17
  168.6 1.7 gather_fusion.3
  170.3 1.3 collective-permute-start.12
  171.7 0.5 collective-permute-start.11
  172.2 1.4 collective-permute-done.10
  173.6 3.6 %collective-permute-done.11 = f32[128,1]{1,0:T(8,128)S(1)} collective-permute-done((f32[128,1]{1,0:T(8,128)S(1)}, f32[128,1]{1,0:T(8,128)S(1)}, u32[]{:S(2)}, u32[]{:S(2)}) %collective-permute-start.11) | collective-permute-done | bytes 544 | tf_op jit(solution)/shard_map/ppermute | solution.py:17
  177.2 0.2 fusion.13
  177.5 0.7 multiply_reduce_fusion.2
  178.2 39.3 %all-reduce.1 = (f32[]{:T(128)}, f32[]{:T(128)}) all-reduce(f32[]{:T(128)} %get-tuple-element.52, f32[]{:T(128)} %get-tuple-element.51), channel_id=1, replica_groups=mesh['lat'=4,'lon'=8] {'lat','lon'}, use_global_device_ids=true, to_apply=%region_9.11 | all-reduce | flops 2 | bytes 16 | tf_op jit(solution)/shard_map/psum | solution.py:35
  221.4 0.1 convert_multiply_fusion
  221.6 10.8 %all-gather.4 = f32[1,2048]{1,0:T(1,128)S(1)} all-gather(f32[1,256]{1,0:T(1,128)S(1)} %get-tuple-element.76), channel_id=6, replica_groups=mesh['lat'=4,'lon'=8] {'lon'}, dimensions={1}, use_global_device_ids=true | all-gather | bytes 9216 | tf_op jit(solution)/shard_map/all_gather | solution.py:58
  232.4 4.2 %collective-permute-start.17 = (f32[1,256]{1,0:T(1,128)S(1)}, f32[1,256]{1,0:T(1,128)S(1)}, u32[]{:S(2)}, u32[]{:S(2)}) collective-permute-start(f32[1,256]{1,0:T(1,128)S(1)} %get-tuple-element.76), channel_id=1, source_target_pairs={{0,8},{8,16},{16,24},{1,9},{9,17},{17,25},{2,10},{10,18},{18,26},{... | collective-permute-start | bytes 3080 | tf_op jit(solution)/shard_map/ppermute | solution.py:17
  236.6 1.7 gather_fusion.4
  238.4 1.3 collective-permute-start.16
  239.7 0.5 collective-permute-start.15
  240.2 1.4 collective-permute-done.14
  241.6 3.6 %collective-permute-done.15 = f32[128,1]{1,0:T(8,128)S(1)} collective-permute-done((f32[128,1]{1,0:T(8,128)S(1)}, f32[128,1]{1,0:T(8,128)S(1)}, u32[]{:S(2)}, u32[]{:S(2)}) %collective-permute-start.15) | collective-permute-done | bytes 544 | tf_op jit(solution)/shard_map/ppermute | solution.py:17
  245.3 0.2 fusion.2
  245.5 0.7 multiply_reduce_fusion
  246.2 40.2 %all-reduce = (f32[]{:T(128)}, f32[]{:T(128)}) all-reduce(f32[]{:T(128)} %get-tuple-element.56, f32[]{:T(128)} %get-tuple-element.55), channel_id=1, replica_groups=mesh['lat'=4,'lon'=8] {'lat','lon'}, use_global_device_ids=true, to_apply=%region_13.15 | all-reduce | flops 2 | bytes 16 | tf_op jit(solution)/shard_map/psum | solution.py:35
  290.5 0.9 multiply_subtract_fusion
  (54 shorter events, 0.9 us)
Async XLA Ops:
  0.6 1.5 copy-start.4
  1.6 36.3 %collective-permute-start.1 = (f32[128,1]{1,0:T(8,128)S(1)}, f32[128,1]{1,0:T(8,128)S(1)}, u32[]{:S(2)}, u32[]{:S(2)}) collective-permute-start(f32[128,1]{1,0:T(8,128)S(1)} %slice.203), channel_id=1, source_target_pairs={{0,1},{1,2},{2,3},{3,4},{4,5},{5,6},{6,7},{7,0},{8,9},{9,10},{10,1... | collective-permute-start | bytes 1544 | tf_op jit(solution)/shard_map/ppermute | solution.py:17
  2.1 4.5 %copy-start = (s32[128,256]{1,0:T(8,128)S(1)}, s32[128,256]{1,0:T(8,128)}, u32[]{:S(2)}) copy-start(s32[128,256]{1,0:T(8,128)} %param.20) | copy-start | bytes 393220
  2.1 4.6 %copy-start.1 = (f32[128,256]{1,0:T(8,128)S(1)}, f32[128,256]{1,0:T(8,128)}, u32[]{:S(2)}) copy-start(f32[128,256]{1,0:T(8,128)} %param.16) | copy-start | bytes 393220
  2.3 41.2 %collective-permute-start.4 = (f32[1,256]{1,0:T(1,128)S(1)}, f32[1,256]{1,0:T(1,128)S(1)}, u32[]{:S(2)}, u32[]{:S(2)}) collective-permute-start(f32[1,256]{1,0:T(1,128)S(1)} %slice.255), channel_id=1, source_target_pairs={{0,8},{8,16},{16,24},{1,9},{9,17},{17,25},{2,10},{10,18},{18,26},{... | collective-permute-start | bytes 3080 | tf_op jit(solution)/shard_map/ppermute | solution.py:17
  6.7 36.7 %collective-permute-start.3 = (f32[1,256]{1,0:T(1,128)S(1)}, f32[1,256]{1,0:T(1,128)S(1)}, u32[]{:S(2)}, u32[]{:S(2)}) collective-permute-start(f32[1,256]{1,0:T(1,128)S(1)} %get-tuple-element.87), channel_id=1, source_target_pairs={{8,0},{16,8},{24,16},{9,1},{17,9},{25,17},{10,2},{18,10},{26,18},{... | collective-permute-start | bytes 3080 | tf_op jit(solution)/shard_map/ppermute | solution.py:19
  8.0 35.5 %collective-permute-start.5 = (f32[1,256]{1,0:T(1,128)S(1)}, f32[1,256]{1,0:T(1,128)S(1)}, u32[]{:S(2)}, u32[]{:S(2)}) collective-permute-start(f32[1,256]{1,0:T(1,128)S(1)} %get-tuple-element.88), channel_id=1, source_target_pairs={{0,8},{8,16},{16,24},{1,9},{9,17},{17,25},{2,10},{10,18},{18,26},{... | collective-permute-start | bytes 3080 | tf_op jit(solution)/shard_map/ppermute | solution.py:17
  12.7 25.7 %collective-permute-start = (f32[128,1]{1,0:T(8,128)S(1)}, f32[128,1]{1,0:T(8,128)S(1)}, u32[]{:S(2)}, u32[]{:S(2)}) collective-permute-start(f32[128,1]{1,0:T(8,128)S(1)} %get-tuple-element.85), channel_id=1, source_target_pairs={{1,0},{2,1},{3,2},{4,3},{5,4},{6,5},{7,6},{0,7},{9,8},{10,9},{11,1... | collective-permute-start | bytes 1544 | tf_op jit(solution)/shard_map/ppermute | solution.py:19
  15.4 10.3 %copy-start.5 = (s32[256]{0:T(256)S(1)}, s32[256]{0:T(256)}, u32[]{:S(2)}) copy-start(s32[256]{0:T(256)} %param.21) | copy-start | bytes 3076
  36.2 7.3 %copy-start.3 = (f32[128,256]{1,0:T(8,128)S(1)}, f32[128,256]{1,0:T(8,128)}, u32[]{:S(2)}) copy-start(f32[128,256]{1,0:T(8,128)} %param.18) | copy-start | bytes 393220
  37.9 5.5 %collective-permute-start.2 = (f32[128,1]{1,0:T(8,128)S(1)}, f32[128,1]{1,0:T(8,128)S(1)}, u32[]{:S(2)}, u32[]{:S(2)}) collective-permute-start(f32[128,1]{1,0:T(8,128)S(1)} %get-tuple-element.86), channel_id=1, source_target_pairs={{0,1},{1,2},{2,3},{3,4},{4,5},{5,6},{6,7},{7,0},{8,9},{9,10},{10,1... | collective-permute-start | bytes 1544 | tf_op jit(solution)/shard_map/ppermute | solution.py:17
  38.3 5.4 %copy-start.2 = (f32[128,256]{1,0:T(8,128)S(1)}, f32[128,256]{1,0:T(8,128)}, u32[]{:S(2)}) copy-start(f32[128,256]{1,0:T(8,128)} %param.17) | copy-start | bytes 393220
  94.6 12.9 %collective-permute-start.9 = (f32[1,256]{1,0:T(1,128)S(1)}, f32[1,256]{1,0:T(1,128)S(1)}, u32[]{:S(2)}, u32[]{:S(2)}) collective-permute-start(f32[1,256]{1,0:T(1,128)S(1)} %get-tuple-element.84), channel_id=1, source_target_pairs={{0,8},{8,16},{16,24},{1,9},{9,17},{17,25},{2,10},{10,18},{18,26},{... | collective-permute-start | bytes 3080 | tf_op jit(solution)/shard_map/ppermute | solution.py:17
  100.6 6.9 %collective-permute-start.8 = (f32[1,256]{1,0:T(1,128)S(1)}, f32[1,256]{1,0:T(1,128)S(1)}, u32[]{:S(2)}, u32[]{:S(2)}) collective-permute-start(f32[1,256]{1,0:T(1,128)S(1)} %get-tuple-element.83), channel_id=1, source_target_pairs={{8,0},{16,8},{24,16},{9,1},{17,9},{25,17},{10,2},{18,10},{26,18},{... | collective-permute-start | bytes 3080 | tf_op jit(solution)/shard_map/ppermute | solution.py:19
  101.9 2.0 collective-permute-start.6
  101.9 5.5 %collective-permute-start.7 = (f32[128,1]{1,0:T(8,128)S(1)}, f32[128,1]{1,0:T(8,128)S(1)}, u32[]{:S(2)}, u32[]{:S(2)}) collective-permute-start(f32[128,1]{1,0:T(8,128)S(1)} %get-tuple-element.82), channel_id=1, source_target_pairs={{0,1},{1,2},{2,3},{3,4},{4,5},{5,6},{6,7},{7,0},{8,9},{9,10},{10,1... | collective-permute-start | bytes 1544 | tf_op jit(solution)/shard_map/ppermute | solution.py:17
  164.3 12.9 %collective-permute-start.13 = (f32[1,256]{1,0:T(1,128)S(1)}, f32[1,256]{1,0:T(1,128)S(1)}, u32[]{:S(2)}, u32[]{:S(2)}) collective-permute-start(f32[1,256]{1,0:T(1,128)S(1)} %get-tuple-element.80), channel_id=1, source_target_pairs={{0,8},{8,16},{16,24},{1,9},{9,17},{17,25},{2,10},{10,18},{18,26},{... | collective-permute-start | bytes 3080 | tf_op jit(solution)/shard_map/ppermute | solution.py:17
  170.3 6.9 %collective-permute-start.12 = (f32[1,256]{1,0:T(1,128)S(1)}, f32[1,256]{1,0:T(1,128)S(1)}, u32[]{:S(2)}, u32[]{:S(2)}) collective-permute-start(f32[1,256]{1,0:T(1,128)S(1)} %get-tuple-element.79), channel_id=1, source_target_pairs={{8,0},{16,8},{24,16},{9,1},{17,9},{25,17},{10,2},{18,10},{26,18},{... | collective-permute-start | bytes 3080 | tf_op jit(solution)/shard_map/ppermute | solution.py:19
  171.6 2.0 collective-permute-start.10
  171.7 5.5 %collective-permute-start.11 = (f32[128,1]{1,0:T(8,128)S(1)}, f32[128,1]{1,0:T(8,128)S(1)}, u32[]{:S(2)}, u32[]{:S(2)}) collective-permute-start(f32[128,1]{1,0:T(8,128)S(1)} %get-tuple-element.78), channel_id=1, source_target_pairs={{0,1},{1,2},{2,3},{3,4},{4,5},{5,6},{6,7},{7,0},{8,9},{9,10},{10,1... | collective-permute-start | bytes 1544 | tf_op jit(solution)/shard_map/ppermute | solution.py:17
  232.4 12.9 %collective-permute-start.17 = (f32[1,256]{1,0:T(1,128)S(1)}, f32[1,256]{1,0:T(1,128)S(1)}, u32[]{:S(2)}, u32[]{:S(2)}) collective-permute-start(f32[1,256]{1,0:T(1,128)S(1)} %get-tuple-element.76), channel_id=1, source_target_pairs={{0,8},{8,16},{16,24},{1,9},{9,17},{17,25},{2,10},{10,18},{18,26},{... | collective-permute-start | bytes 3080 | tf_op jit(solution)/shard_map/ppermute | solution.py:17
  238.4 6.9 %collective-permute-start.16 = (f32[1,256]{1,0:T(1,128)S(1)}, f32[1,256]{1,0:T(1,128)S(1)}, u32[]{:S(2)}, u32[]{:S(2)}) collective-permute-start(f32[1,256]{1,0:T(1,128)S(1)} %get-tuple-element.75), channel_id=1, source_target_pairs={{8,0},{16,8},{24,16},{9,1},{17,9},{25,17},{10,2},{18,10},{26,18},{... | collective-permute-start | bytes 3080 | tf_op jit(solution)/shard_map/ppermute | solution.py:19
  239.7 2.0 collective-permute-start.14
  239.7 5.5 %collective-permute-start.15 = (f32[128,1]{1,0:T(8,128)S(1)}, f32[128,1]{1,0:T(8,128)S(1)}, u32[]{:S(2)}, u32[]{:S(2)}) collective-permute-start(f32[128,1]{1,0:T(8,128)S(1)} %get-tuple-element.74), channel_id=1, source_target_pairs={{0,1},{1,2},{2,3},{3,4},{4,5},{5,6},{6,7},{7,0},{8,9},{9,10},{10,1... | collective-permute-start | bytes 1544 | tf_op jit(solution)/shard_map/ppermute | solution.py:17
where the time goes:
time: 293 us; the launch traced here: 291 us
  blocking collectives  209 us (71%)
  starting transfers between devices  31.9 us (11%)
  waiting for transfers between devices  20.3 us (7%)
  between operations  14.9 us (5%)
  local copies, waits for them, and re-layouts  10.1 us (3%)
  other arithmetic  4.81 us (2%)
    psum x4, blocking collectives, paired(): lax.psum((jnp.sum(residual * residual), jnp.sum(residual * image)), ('lat...  158 us
    all_gather x5, blocking collectives, mirror_row(): whole_row = lax.all_gather(top_values, 'lon', axis=0, tiled=True)  51.3 us
    ppermute x10, starting transfers between devices, with_halo(): lax.ppermute(tail, axis, [(i, (i + 1) % count) for i in range(ends)])  23.9 us
    ppermute x10, waiting for transfers between devices, with_halo(): lax.ppermute(tail, axis, [(i, (i + 1) % count) for i in range(ends)])  16.1 us
    gather x5, local copies, waits for them, and re-layouts, mirror_row(): return jnp.take(whole_row, fold_partner, axis=0)  8.62 us
    ppermute x8, starting transfers between devices, with_halo(): lax.ppermute(head, axis, [((i + 1) % count, i) for i in range(ends)])  8.03 us
  transfers between devices with their start and end apart: 18, of which 7 were waited for; matrix products, arithmetic and copies ran while one was open for 3% of the time, Pallas kernels for 0%

commit v1 on v0

v1 whole, which is shorter than its diff:
```python
import jax
import jax.numpy as jnp
from jax import lax
from jax.experimental import pallas as pl
from jax.experimental.pallas import tpu as pltpu
from jax.sharding import PartitionSpec as P

ITERS = 4
MESH = pl.DeviceIdType.MESH
NORTH, SOUTH, EAST, WEST = range(4)
f32 = jnp.float32


def kernel(lats, lons, rhs_hbm, diag_hbm, east_hbm, north_hbm, land_hbm, partner_hbm,
           sol_ref, res_ref,
           rhs, diag, east, north, land, partner, load_sem,
           held, cols_out, rows_in, cols_in, coef_cols, coef_rows, coef_cols_in,
           send_sem, recv_sem, coef_send, coef_recv,
           part_out, part_in, part_send, part_recv):
    rows, cols = rhs.shape
    count = lats * lons
    lat, lon = lax.axis_index("lat"), lax.axis_index("lon")
    me = lat * lons + lon
    on_top, on_bottom = lat == lats - 1, lat == 0

    loads = [
        pltpu.make_async_copy(src, dst, load_sem.at[i])
        for i, (src, dst) in enumerate(
            ((rhs_hbm, rhs), (land_hbm, land), (east_hbm, east), (north_hbm, north),
             (partner_hbm, partner), (diag_hbm, diag)))
    ]
    for load in loads:
        load.start()

    barrier = pltpu.get_barrier_semaphore()

    def device(shift):
        other = lax.rem(me + shift, count)
        return (other // lons, lax.rem(other, lons))

    def greet(shift, carry):
        pl.semaphore_signal(barrier, inc=1, device_id=device(shift), device_id_type=MESH)
        return carry

    lax.fori_loop(1, count, greet, 0)

    east_id = (lat, lax.rem(lon + 1, lons))
    west_id = (lat, lax.rem(lon + lons - 1, lons))
    north_id = (lax.rem(lat + 1, lats), lon)
    south_id = (lax.rem(lat + lats - 1, lats), lon)
    fold_id = (lat, lons - 1 - lon)

    row_ids = lax.broadcasted_iota(jnp.int32, (rows, cols), 0)
    col_ids = lax.broadcasted_iota(jnp.int32, (rows, cols), 1)
    eye = lax.broadcasted_iota(jnp.int32, (rows, rows), 0) == lax.broadcasted_iota(
        jnp.int32, (rows, rows), 1)
    lane = lax.broadcasted_iota(jnp.int32, (1, 128), 1)

    def flat(column):
        return jnp.sum(jnp.where(eye, column, 0.0), axis=0, keepdims=True)

    def upright(row):
        return jnp.sum(jnp.where(eye, row, 0.0), axis=1, keepdims=True)

    for load in loads:
        load.wait()
    ocean = land[...].astype(f32)
    east_c = east[...]
    coef_cols[...] = jnp.broadcast_to(flat(east_c[:, cols - 1:]), (8, rows))
    held[0] = ocean * rhs[...]

    own = lax.rem(partner[...], cols)
    lower = jnp.broadcast_to(lax.rem(own, 128), (8, cols))
    panel = jnp.broadcast_to(own // 128, (8, cols))

    def mirrored(block):
        pieces = []
        for at in range(0, cols, 128):
            index = lower[:, at:at + 128]
            which = panel[:, at:at + 128]
            picked = jnp.zeros((8, 128), f32)
            for k in range(cols // 128):
                found = jnp.take_along_axis(block[:, k * 128:(k + 1) * 128], index, axis=1)
                picked = jnp.where(which == k, found, picked)
            pieces.append(picked)
        return jnp.concatenate(pieces, axis=1)[7:8]

    @pl.when(on_bottom)
    def _():
        for k in range(ITERS):
            rows_in[k, SOUTH] = jnp.zeros((8, cols), f32)
        coef_rows[1] = jnp.zeros((8, cols), f32)

    pl.semaphore_wait(barrier, count - 1)

    def remote(src, dst, send, recv, to):
        return pltpu.make_async_remote_copy(
            src_ref=src, dst_ref=dst, send_sem=send, recv_sem=recv,
            device_id=to, device_id_type=MESH)

    def halo_copies(k):
        top, base = held.at[k, pl.ds(rows - 8, 8)], held.at[k, pl.ds(0, 8)]
        sems = lambda way: (send_sem.at[k, way], recv_sem.at[k, way])
        to_east = remote(cols_out.at[k, 0], cols_in.at[k, 0], *sems(WEST), east_id)
        to_west = remote(cols_out.at[k, 1], cols_in.at[k, 1], *sems(EAST), west_id)
        to_fold = remote(top, rows_in.at[k, NORTH], *sems(NORTH), fold_id)
        to_north = remote(top, rows_in.at[k, SOUTH], send_sem.at[k, NORTH], recv_sem.at[k, SOUTH], north_id)
        to_south = remote(base, rows_in.at[k, NORTH], send_sem.at[k, SOUTH], recv_sem.at[k, NORTH], south_id)
        return to_east, to_west, to_fold, to_north, to_south

    coef_east = remote(coef_cols, coef_cols_in, coef_send.at[0], coef_recv.at[0], east_id)
    coef_top = north.at[pl.ds(rows - 8, 8)]
    coef_fold = remote(coef_top, coef_rows.at[0], coef_send.at[1], coef_recv.at[1], fold_id)
    coef_north = remote(coef_top, coef_rows.at[1], coef_send.at[1], coef_recv.at[2], north_id)

    coef_east.start()

    @pl.when(on_top)
    def _():
        coef_fold.start()

    @pl.when(jnp.logical_not(on_top))
    def _():
        coef_north.start()

    def send_halo(k):
        to_east, to_west, to_fold, to_north, to_south = halo_copies(k)

        @pl.when(on_top)
        def _():
            to_fold.start()

        @pl.when(jnp.logical_not(on_top))
        def _():
            to_north.start()

        @pl.when(jnp.logical_not(on_bottom))
        def _():
            to_south.start()

        masked = held[k]
        cols_out[k, 0] = jnp.broadcast_to(flat(masked[:, cols - 1:]), (8, rows))
        cols_out[k, 1] = jnp.broadcast_to(flat(masked[:, :1]), (8, rows))
        to_east.start()
        to_west.start()

    def take_halo(k):
        to_east, to_west, to_fold, to_north, to_south = halo_copies(k)
        to_east.wait_recv()
        to_west.wait_recv()
        to_south.wait_recv()

        @pl.when(jnp.logical_not(on_bottom))
        def _():
            to_north.wait_recv()

    def end_halo(k):
        to_east, to_west, to_fold, to_north, to_south = halo_copies(k)
        to_east.wait_send()
        to_west.wait_send()
        to_north.wait_send()

        @pl.when(jnp.logical_not(on_bottom))
        def _():
            to_south.wait_send()

    def part_copy(which, shift):
        return remote(part_out.at[which], part_in.at[which, shift - 1],
                      part_send.at[which], part_recv.at[which], device(shift))

    def share(which, values):
        packed = jnp.zeros((1, 128), f32)
        for k, value in enumerate(values):
            packed = jnp.where(lane == k, value, packed)
        part_out[which] = packed

        def send(shift, carry):
            part_copy(which, shift).start()
            return carry

        lax.fori_loop(1, count, send, 0)
        return packed

    def gathered(which):
        whole = part_in.at[which]
        pltpu.make_async_copy(whole, whole, part_recv.at[which]).wait()
        return jnp.sum(part_in[which], axis=0)

    def dot(a, b):
        return jnp.sum(jnp.sum(a * b, axis=0, keepdims=True), axis=1, keepdims=True)

    def pick(packed, k):
        return packed[:, k:k + 1]

    send_halo(0)
    take_halo(0)
    coef_east.wait_recv()

    @pl.when(on_top)
    def _():
        coef_fold.wait_recv()

    @pl.when(jnp.logical_not(on_bottom))
    def _():
        coef_north.wait_recv()

    top_flag = jnp.where(on_top, 1, 0)
    is_top = jnp.full((1, cols), top_flag, jnp.int32) == 1
    north_c = north[...]
    coef_mirror = jnp.where(is_top, coef_rows[0], 0.0)
    fold_c = 0.5 * (north_c[rows - 1:] + mirrored(coef_mirror))
    north_c = jnp.where(
        row_ids == rows - 1, jnp.where(is_top, fold_c, north_c[rows - 1:]), north_c)
    west_c = jnp.where(
        col_ids == 0, upright(coef_cols_in[:1]), pltpu.roll(east_c, 1, 1))
    south_c = jnp.where(row_ids == 0, coef_rows[1][7:8], pltpu.roll(north_c, 1, 0))
    east_c, west_c = ocean * east_c, ocean * west_c
    north_c, south_c = ocean * north_c, ocean * south_c
    centre = diag[...] + ((east_c + west_c) + (north_c + south_c))

    def operate(k, field):
        masked = held[k]
        block = rows_in[k, NORTH]
        above = jnp.where(is_top, mirrored(block), block[:1])
        below = rows_in[k, SOUTH][7:8]
        east_v = jnp.where(col_ids == cols - 1, upright(cols_in[k, 1][:1]), pltpu.roll(masked, cols - 1, 1))
        west_v = jnp.where(col_ids == 0, upright(cols_in[k, 0][:1]), pltpu.roll(masked, 1, 1))
        north_v = jnp.where(row_ids == rows - 1, above, pltpu.roll(masked, rows - 1, 0))
        south_v = jnp.where(row_ids == 0, below, pltpu.roll(masked, 1, 0))
        return centre * field - (
            (east_c * east_v + west_c * west_v) + (north_c * north_v + south_c * south_v))

    v0 = rhs[...]
    image = operate(0, v0)
    held[1] = ocean * image
    send_halo(1)
    packed = share(0, (dot(v0, v0), dot(v0, image), dot(image, image)))
    take_halo(1)
    second = operate(1, image)
    packed = packed + gathered(0)
    norm = pick(packed, 0)
    shift = pick(packed, 1) / norm
    spread = pick(packed, 2) / norm - shift * shift
    sigma = jnp.sqrt(jnp.maximum(spread, 1e-4 * shift * shift))
    scale = 1.0 / sigma
    v1 = (image - shift * v0) * scale
    v2 = ((second - shift * image) * scale - shift * v1) * scale - v0
    held[2] = ocean * v2
    send_halo(2)
    take_halo(2)
    v3 = (operate(2, v2) - shift * v2) * scale - v1
    held[3] = ocean * v3
    send_halo(3)
    take_halo(3)
    v4 = (operate(3, v3) - shift * v3) * scale - v2

    basis = (v0, v1, v2, v3, v4)
    pairs = [(i, j) for j in range(ITERS + 1) for i in range(j + 1) if i < ITERS]
    packed = share(1, [dot(basis[i], basis[j]) for i, j in pairs])
    packed = packed + gathered(1)
    gram = {}
    for k, (i, j) in enumerate(pairs):
        gram[i, j] = gram[j, i] = pick(packed, k)

    def inner(a, b):
        total = None
        for i, x in enumerate(a):
            line = None
            for j, y in enumerate(b):
                term = gram[i, j] * y
                line = term if line is None else line + term
            total = x * line if total is None else total + x * line
        return total

    def image_of(a):
        out = []
        for k in range(len(a) + 1):
            term = shift * a[k] if k < len(a) else None
            for near in (k - 1, k + 1):
                if 0 <= near < len(a):
                    term = sigma * a[near] if term is None else term + sigma * a[near]
            out.append(term)
        return out

    one = jnp.ones((1, 1), f32)
    left, way, found = [one], [one], []
    rr = inner(left, left)
    for step in range(ITERS):
        along = image_of(way)
        alpha = rr / inner(way, along)
        found = [(found[k] + alpha * w) if k < len(found) else alpha * w for k, w in enumerate(way)]
        left = [(left[k] - alpha * a) if k < len(left) else -alpha * a for k, a in enumerate(along)]
        if step + 1 < ITERS:
            new = inner(left, left)
            ratio = new / rr
            way = [(left[k] + ratio * way[k]) if k < len(way) else left[k] for k in range(len(left))]
            rr = new

    def mix(weights):
        total = weights[0] * basis[0]
        for weight, vector in zip(weights[1:], basis[1:]):
            total = total + weight * vector
        return total

    sol_ref[...] = mix(found)
    res_ref[...] = mix(left)

    for k in range(ITERS):
        end_halo(k)
    coef_east.wait_send()
    coef_fold.wait_send()
    for which in range(2):
        whole = part_in.at[which]
        pltpu.make_async_copy(whole, whole, part_send.at[which]).wait()


def solution(mesh):
    lats, lons = mesh.shape["lat"], mesh.shape["lon"]
    count = lats * lons

    def local(right_side, diagonal, east_coef, north_coef, land_sea, fold_partner):
        rows, cols = right_side.shape
        block = lambda dtype=f32: pltpu.VMEM((rows, cols), dtype)
        dma = pltpu.SemaphoreType.DMA
        return pl.pallas_call(
            lambda *refs: kernel(lats, lons, *refs),
            out_shape=(jax.ShapeDtypeStruct((rows, cols), f32),) * 2,
            in_specs=[pl.BlockSpec(memory_space=pl.ANY)] * 6,
            out_specs=(pl.BlockSpec(memory_space=pltpu.VMEM),) * 2,
            scratch_shapes=[
                block(), block(), block(), block(), block(jnp.int32),
                pltpu.VMEM((1, cols), jnp.int32), dma((6,)),
                pltpu.VMEM((ITERS, rows, cols), f32),
                pltpu.VMEM((ITERS, 2, 8, rows), f32),
                pltpu.VMEM((ITERS, 2, 8, cols), f32),
                pltpu.VMEM((ITERS, 2, 8, rows), f32),
                pltpu.VMEM((8, rows), f32),
                pltpu.VMEM((2, 8, cols), f32),
                pltpu.VMEM((8, rows), f32),
                dma((ITERS, 4)), dma((ITERS, 4)), dma((2,)), dma((3,)),
                pltpu.VMEM((2, 1, 128), f32),
                pltpu.VMEM((2, count - 1, 1, 128), f32),
                dma((2,)), dma((2,)),
            ],
            compiler_params=pltpu.CompilerParams(collective_id=0, has_side_effects=True),
            name="cg",
        )(right_side, diagonal, east_coef, north_coef, land_sea, fold_partner.reshape(1, cols))

    placed = (P("lat", "lon"),) * 5 + (P("lon"),)
    return jax.shard_map(
        local, mesh=mesh, in_specs=placed,
        out_specs=(P("lat", "lon"), P("lat", "lon")), check_vma=False)
```

time: 293 us -> 33.3 us (0.11)
  blocking collectives: 209 us -> 0 us
  starting transfers between devices: 31.9 us -> 0 us
  Pallas kernels: 0 us -> 30.2 us
  waiting for transfers between devices: 20.3 us -> 0 us
  between operations: 14.9 us -> 0.65 us
  local copies, waits for them, and re-layouts: 10.1 us -> 2.26 us
  other arithmetic: 4.81 us -> 0 us
    psum x4 -> x0, blocking collectives: 158 us -> none  [paired(): lax.psum((jnp.sum(residual * residual), jnp.sum(residual * image)), ('lat...]
    all_gather x5 -> x0, blocking collectives: 51.3 us -> none  [mirror_row(): whole_row = lax.all_gather(top_values, 'lon', axis=0, tiled=True)]
    ppermute x18 -> x0, starting transfers between devices: 31.9 us -> none  [the longest x10 23.9 us: with_halo(): lax.ppermute(tail, axis, [(i, (i + 1) % count) for i in range(ends)])]
    pallas_call x0 -> x1, Pallas kernels: none -> 30.2 us  [local(): pl.pallas_call(lambda *refs: kernel(lats, lons, *refs), out_shape=(jax.Sh...]
    ppermute x18 -> x0, waiting for transfers between devices: 20.3 us -> none  [the longest x10 16.1 us: with_halo(): lax.ppermute(tail, axis, [(i, (i + 1) % count) for i in range(ends)])]
    gather x5 -> x0, local copies, waits for them, and re-layouts: 8.62 us -> none  [mirror_row(): return jnp.take(whole_row, fold_partner, axis=0)]
  transfers between devices with their start and end apart: 18 -> 0, of which waited for: 7 -> 0; matrix products, arithmetic and copies ran while one was open for 3% -> 0% of each run, Pallas kernels for 0% -> 0%
where the time goes in v1:
time: 33.3 us; the launch traced here: 33.1 us
  Pallas kernels  30.2 us (91%)
  local copies, waits for them, and re-layouts  2.26 us (7%)
  between operations  0.65 us (2%)
    pallas_call x1, Pallas kernels, local(): pl.pallas_call(lambda *refs: kernel(lats, lons, *refs), out_shape=(jax.Sh...  30.2 us
    unnamed x4, local copies, waits for them, and re-layouts  2.26 us

profile of v1, /device:TPU:0, one launch (start us, length us, event | category | flops | bytes accessed | tf_op | source)
XLA Modules:
  0.0 33.1 jit_solution(13599308229403751844)
XLA Ops:
  0.6 30.2 %cg.1 = (f32[128,256]{1,0:T(8,128)}, f32[128,256]{1,0:T(8,128)}) custom-call(f32[128,256]{1,0:T(8,128)} %refs_0_.1, f32[128,256]{1,0:T(8,128)} %refs_1_.1, f32[128,256]{1,0:T(8,128)} %refs_2_.1, f32[128,256]{1,0:T(8,128)} %refs_3_.1, s32[128,256]{1,0:T(8,128)} %refs_4_.1, s32[1,256]{1,0:T(1,128)} %bitcast.1), custom_call_target="tpu_custom_call" | custom-call | tf_op jit(solution)/shard_map/cg/pallas_call | solution.py:325
  30.9 0.0 copy-start
  30.9 1.6 %copy.10 = f32[128,256]{1,0:T(8,128)} copy(f32[128,256]{1,0:T(8,128)} %get-tuple-element.4) | data formatting | bytes 262144
  32.5 0.0 copy-done
  32.5 0.7 %copy.11 = f32[128,256]{1,0:T(8,128)} copy(f32[128,256]{1,0:T(8,128)S(1)} %copy-done) | data formatting | bytes 262144
Async XLA Ops:
  30.9 1.6 %copy-start = (f32[128,256]{1,0:T(8,128)S(1)}, f32[128,256]{1,0:T(8,128)}, u32[]{:S(2)}) copy-start(f32[128,256]{1,0:T(8,128)} %get-tuple-element.5) | copy-start | bytes 393220

commit v2 on v1

--- a/solution.py
+++ b/solution.py
@@ -12,7 +12,7 @@
 
 
 def kernel(lats, lons, rhs_hbm, diag_hbm, east_hbm, north_hbm, land_hbm, partner_hbm,
-           sol_ref, res_ref,
+           v0_ref, v1_ref, v2_ref, v3_ref, v4_ref, mix_ref,
            rhs, diag, east, north, land, partner, load_sem,
            held, cols_out, rows_in, cols_in, coef_cols, coef_rows, coef_cols_in,
            send_sem, recv_sem, coef_send, coef_recv,
@@ -253,6 +253,11 @@
     send_halo(3)
     take_halo(3)
     v4 = (operate(3, v3) - shift * v3) * scale - v2
+    v0_ref[...] = v0
+    v1_ref[...] = v1
+    v2_ref[...] = v2
+    v3_ref[...] = v3
+    v4_ref[...] = v4
 
     basis = (v0, v1, v2, v3, v4)
     pairs = [(i, j) for j in range(ITERS + 1) for i in range(j + 1) if i < ITERS]
@@ -296,14 +301,14 @@
             way = [(left[k] + ratio * way[k]) if k < len(way) else left[k] for k in range(len(left))]
             rr = new
 
-    def mix(weights):
-        total = weights[0] * basis[0]
-        for weight, vector in zip(weights[1:], basis[1:]):
-            total = total + weight * vector
-        return total
-
-    sol_ref[...] = mix(found)
-    res_ref[...] = mix(left)
+    weights = jnp.zeros((8, 128), f32)
+    spot = 128 * lax.broadcasted_iota(jnp.int32, (8, 128), 0) + lax.broadcasted_iota(
+        jnp.int32, (8, 128), 1)
+    for k, weight in enumerate(found):
+        weights = jnp.where(spot == k, weight, weights)
+    for k, weight in enumerate(left):
+        weights = jnp.where(spot == 128 + k, weight, weights)
+    mix_ref[...] = weights
 
     for k in range(ITERS):
         end_halo(k)
@@ -314,6 +319,15 @@
         pltpu.make_async_copy(whole, whole, part_send.at[which]).wait()
 
 
+def combine(v0_ref, v1_ref, v2_ref, v3_ref, v4_ref, mix_ref, sol_ref, res_ref):
+    basis = [ref[...] for ref in (v0_ref, v1_ref, v2_ref, v3_ref, v4_ref)]
+    for line, size, out_ref in ((0, ITERS, sol_ref), (1, ITERS + 1, res_ref)):
+        total = mix_ref[line:line + 1, 0:1] * basis[0]
+        for k in range(1, size):
+            total = total + mix_ref[line:line + 1, k:k + 1] * basis[k]
+        out_ref[...] = total
+
+
 def solution(mesh):
     lats, lons = mesh.shape["lat"], mesh.shape["lon"]
     count = lats * lons
@@ -322,11 +336,11 @@
         rows, cols = right_side.shape
         block = lambda dtype=f32: pltpu.VMEM((rows, cols), dtype)
         dma = pltpu.SemaphoreType.DMA
-        return pl.pallas_call(
+        *basis, weights = pl.pallas_call(
             lambda *refs: kernel(lats, lons, *refs),
-            out_shape=(jax.ShapeDtypeStruct((rows, cols), f32),) * 2,
+            out_shape=(pltpu.VMEM((rows, cols), f32),) * (ITERS + 1) + (pltpu.VMEM((8, 128), f32),),
             in_specs=[pl.BlockSpec(memory_space=pl.ANY)] * 6,
-            out_specs=(pl.BlockSpec(memory_space=pltpu.VMEM),) * 2,
+            out_specs=(pl.BlockSpec(memory_space=pltpu.VMEM),) * (ITERS + 2),
             scratch_shapes=[
                 block(), block(), block(), block(), block(jnp.int32),
                 pltpu.VMEM((1, cols), jnp.int32), dma((6,)),
@@ -346,6 +360,14 @@
             name="cg",
         )(right_side, diagonal, east_coef, north_coef, land_sea, fold_partner.reshape(1, cols))
 
+        return pl.pallas_call(
+            combine,
+            out_shape=(jax.ShapeDtypeStruct((rows, cols), f32),) * 2,
+            in_specs=[pl.BlockSpec(memory_space=pltpu.VMEM)] * (ITERS + 2),
+            out_specs=(pl.BlockSpec(memory_space=pltpu.VMEM),) * 2,
+            name="combine",
+        )(*[pltpu.with_memory_space_constraint(x, pltpu.VMEM) for x in (*basis, weights)])
+
     placed = (P("lat", "lon"),) * 5 + (P("lon"),)
     return jax.shard_map(
         local, mesh=mesh, in_specs=placed,

time: 33.3 us -> 31.1 us (0.934)
  local copies, waits for them, and re-layouts: 2.26 us -> 0 us
    unnamed x4 -> x0, local copies, waits for them, and re-layouts: 2.26 us -> none
    pallas_call x1 -> x2, Pallas kernels: 30.2 us -> 30.3 us  [the longest x1 29.5 us: local(): pl.pallas_call(lambda *refs: kernel(lats, lons, *refs), out_shape=(pltpu....]
where the time goes in v2:
time: 31.1 us; the launch traced here: 31 us
  Pallas kernels  30.3 us (97%)
  between operations  0.64 us (2%)
    pallas_call x1, Pallas kernels, local(): pl.pallas_call(lambda *refs: kernel(lats, lons, *refs), out_shape=(pltpu....  29.5 us
    pallas_call x1, Pallas kernels, local(): pl.pallas_call(combine, out_shape=(jax.ShapeDtypeStruct((rows, cols), f32...  0.85 us

profile of v2, /device:TPU:0, one launch (start us, length us, event | category | flops | bytes accessed | tf_op | source)
XLA Modules:
  0.0 31.0 jit_solution(4729043221213017672)
XLA Ops:
  0.6 29.5 %cg.1 = (f32[128,256]{1,0:T(8,128)S(1)}, f32[128,256]{1,0:T(8,128)S(1)}, f32[128,256]{1,0:T(8,128)S(1)}, f32[128,256]{1,0:T(8,128)S(1)}, f32[128,256]{1,0:T(8,128)S(1)}, /*index=5*/f32[8,128]{1,0:T(8,128)S(1)}) custom-call(f32[128,256]{1,0:T(8,128)} %refs_0_.1, f32[128,256]{1,0:T(8,128)} %refs_1_.1, f32[128,256]{1,0:T(8,128)} %refs_2_.1, ...), custom_call_target="tpu_custom_call" | custom-call | tf_op jit(solution)/shard_map/cg/pallas_call | solution.py:339
  30.1 0.8 %combine.1 = (f32[128,256]{1,0:T(8,128)}, f32[128,256]{1,0:T(8,128)}) custom-call(f32[128,256]{1,0:T(8,128)S(1)} %get-tuple-element.8.v0_ref, f32[128,256]{1,0:T(8,128)S(1)} %get-tuple-element.9.v1_ref, f32[128,256]{1,0:T(8,128)S(1)} %get-tuple-element.10.v2_ref, f32[128,256]{1,0:T(8,128)S(1)} %get-tuple-element.11.v3_ref, ...), custom_call_target="tpu_custom_call" | custom-call | tf_op jit(solution)/shard_map/combine/pallas_call | solution.py:363

commit v3 on v2

--- a/solution.py
+++ b/solution.py
@@ -67,7 +67,33 @@
     ocean = land[...].astype(f32)
     east_c = east[...]
     coef_cols[...] = jnp.broadcast_to(flat(east_c[:, cols - 1:]), (8, rows))
-    held[0] = ocean * rhs[...]
+    v0 = rhs[...]
+    masked = ocean * v0
+    held[0] = masked
+    north_c = north[...]
+
+    def rolled(field):
+        return (pltpu.roll(field, cols - 1, 1), pltpu.roll(field, 1, 1),
+                pltpu.roll(field, rows - 1, 0), pltpu.roll(field, 1, 0))
+
+    def dot(a, b):
+        return jnp.sum(jnp.sum(a * b, axis=0, keepdims=True), axis=1, keepdims=True)
+
+    def pick(packed, k):
+        return packed[:, k:k + 1]
+
+    def pack(values):
+        packed = jnp.zeros((1, 128), f32)
+        for k, value in enumerate(values):
+            packed = jnp.where(lane == k, value, packed)
+        return packed
+
+    west_raw, south_raw = pltpu.roll(east_c, 1, 1), pltpu.roll(north_c, 1, 0)
+    guess = diag[...] * v0
+    for coef, other in zip((east_c, west_raw, north_c, south_raw), rolled(masked)):
+        guess = guess + ocean * (coef * (masked - other))
+    guessed = pack((dot(v0, v0), dot(v0, guess), dot(guess, guess)))
+    part_out[0] = guessed
 
     own = lax.rem(partner[...], cols)
     lower = jnp.broadcast_to(lax.rem(own, 128), (8, cols))
@@ -168,31 +194,20 @@
         return remote(part_out.at[which], part_in.at[which, shift - 1],
                       part_send.at[which], part_recv.at[which], device(shift))
 
-    def share(which, values):
-        packed = jnp.zeros((1, 128), f32)
-        for k, value in enumerate(values):
-            packed = jnp.where(lane == k, value, packed)
-        part_out[which] = packed
-
+    def share(which):
         def send(shift, carry):
             part_copy(which, shift).start()
             return carry
 
         lax.fori_loop(1, count, send, 0)
-        return packed
 
     def gathered(which):
         whole = part_in.at[which]
         pltpu.make_async_copy(whole, whole, part_recv.at[which]).wait()
         return jnp.sum(part_in[which], axis=0)
 
-    def dot(a, b):
-        return jnp.sum(jnp.sum(a * b, axis=0, keepdims=True), axis=1, keepdims=True)
-
-    def pick(packed, k):
-        return packed[:, k:k + 1]
-
     send_halo(0)
+    share(0)
     take_halo(0)
     coef_east.wait_recv()
 
@@ -206,66 +221,89 @@
 
     top_flag = jnp.where(on_top, 1, 0)
     is_top = jnp.full((1, cols), top_flag, jnp.int32) == 1
-    north_c = north[...]
     coef_mirror = jnp.where(is_top, coef_rows[0], 0.0)
     fold_c = 0.5 * (north_c[rows - 1:] + mirrored(coef_mirror))
     north_c = jnp.where(
         row_ids == rows - 1, jnp.where(is_top, fold_c, north_c[rows - 1:]), north_c)
-    west_c = jnp.where(
-        col_ids == 0, upright(coef_cols_in[:1]), pltpu.roll(east_c, 1, 1))
-    south_c = jnp.where(row_ids == 0, coef_rows[1][7:8], pltpu.roll(north_c, 1, 0))
-    east_c, west_c = ocean * east_c, ocean * west_c
-    north_c, south_c = ocean * north_c, ocean * south_c
+    west_c = ocean * jnp.where(col_ids == 0, upright(coef_cols_in[:1]), west_raw)
+    south_c = ocean * jnp.where(row_ids == 0, coef_rows[1][7:8], south_raw)
+    east_c, north_c = ocean * east_c, ocean * north_c
     centre = diag[...] + ((east_c + west_c) + (north_c + south_c))
-
-    def operate(k, field):
-        masked = held[k]
+    last_panel = slice(cols - 128, cols)
+    east_edge = jnp.where(col_ids == cols - 1, east_c, 0.0)[:, last_panel]
+    west_edge = jnp.where(col_ids == 0, west_c, 0.0)[:, :128]
+    north_edge, south_edge = north_c[rows - 1:], south_c[:1]
+    inside = (jnp.where(col_ids == cols - 1, 0.0, east_c),
+              jnp.where(col_ids == 0, 0.0, west_c),
+              jnp.where(row_ids == rows - 1, 0.0, north_c),
+              jnp.where(row_ids == 0, 0.0, south_c))
+    base_row = jnp.where(row_ids == 0, 1.0, 0.0)[:8]
+    top_row = jnp.where(row_ids == rows - 1, 1.0, 0.0)[rows - 8:]
+
+    def interior(k, field):
+        terms = [coef * other for coef, other in zip(inside, rolled(held[k]))]
+        return centre * field - ((terms[0] + terms[1]) + (terms[2] + terms[3]))
+
+    def with_edges(k, image):
         block = rows_in[k, NORTH]
         above = jnp.where(is_top, mirrored(block), block[:1])
         below = rows_in[k, SOUTH][7:8]
-        east_v = jnp.where(col_ids == cols - 1, upright(cols_in[k, 1][:1]), pltpu.roll(masked, cols - 1, 1))
-        west_v = jnp.where(col_ids == 0, upright(cols_in[k, 0][:1]), pltpu.roll(masked, 1, 1))
-        north_v = jnp.where(row_ids == rows - 1, above, pltpu.roll(masked, rows - 1, 0))
-        south_v = jnp.where(row_ids == 0, below, pltpu.roll(masked, 1, 0))
-        return centre * field - (
-            (east_c * east_v + west_c * west_v) + (north_c * north_v + south_c * south_v))
-
-    v0 = rhs[...]
-    image = operate(0, v0)
+        image = jnp.concatenate([
+            image[:8] - base_row * (south_edge * below),
+            image[8:rows - 8],
+            image[rows - 8:] - top_row * (north_edge * above)], axis=0)
+        return jnp.concatenate([
+            image[:, :128] - west_edge * upright(cols_in[k, 0][:1]),
+            *([image[:, 128:cols - 128]] if cols > 256 else []),
+            image[:, last_panel] - east_edge * upright(cols_in[k, 1][:1])], axis=1)
+
+    image = with_edges(0, interior(0, v0))
     held[1] = ocean * image
     send_halo(1)
-    packed = share(0, (dot(v0, v0), dot(v0, image), dot(image, image)))
-    take_halo(1)
-    second = operate(1, image)
-    packed = packed + gathered(0)
+    packed = guessed + gathered(0)
     norm = pick(packed, 0)
     shift = pick(packed, 1) / norm
     spread = pick(packed, 2) / norm - shift * shift
     sigma = jnp.sqrt(jnp.maximum(spread, 1e-4 * shift * shift))
     scale = 1.0 / sigma
     v1 = (image - shift * v0) * scale
-    v2 = ((second - shift * image) * scale - shift * v1) * scale - v0
+    second = interior(1, image) - shift * image
+    v0_ref[...] = v0
+    v1_ref[...] = v1
+    base2 = (second * scale - shift * v1) * scale - v0
+    early = [dot(v0, v0), dot(v0, v1)]
+    take_halo(1)
+    v2 = base2 + with_edges(1, jnp.zeros_like(v0)) * (scale * scale)
     held[2] = ocean * v2
     send_halo(2)
+    v2_ref[...] = v2
+    base3 = (interior(2, v2) - shift * v2) * scale - v1
+    early += [dot(v0, v2), dot(v2, v2)]
     take_halo(2)
-    v3 = (operate(2, v2) - shift * v2) * scale - v1
+    v3 = base3 + with_edges(2, jnp.zeros_like(v0)) * scale
     held[3] = ocean * v3
     send_halo(3)
+    v3_ref[...] = v3
+    base4 = (interior(3, v3) - shift * v3) * scale - v2
+    early += [dot(v0, v3), dot(v2, v3), dot(v3, v3)]
+    early = pack(early)
     take_halo(3)
-    v4 = (operate(3, v3) - shift * v3) * scale - v2
-    v0_ref[...] = v0
-    v1_ref[...] = v1
-    v2_ref[...] = v2
-    v3_ref[...] = v3
+    v4 = base4 + with_edges(3, jnp.zeros_like(v0)) * scale
+    packed = jnp.where(lane == 7, dot(v3, v4), early)
+    part_out[1] = packed
+    share(1)
     v4_ref[...] = v4
-
-    basis = (v0, v1, v2, v3, v4)
-    pairs = [(i, j) for j in range(ITERS + 1) for i in range(j + 1) if i < ITERS]
-    packed = share(1, [dot(basis[i], basis[j]) for i, j in pairs])
     packed = packed + gathered(1)
+
+    p00, p01, p02, p22, p03, p23, p33, p34 = [pick(packed, k) for k in range(8)]
+    moment = [p00, p01, p02, p03, p22 - p00 - p02, p23 - p01 - p03]
+    moment.append(p33 - p00 - p02 - moment[4])
+    moment.append(p34 - p01 - p03 - moment[5])
     gram = {}
-    for k, (i, j) in enumerate(pairs):
-        gram[i, j] = gram[j, i] = pick(packed, k)
+    for i in range(ITERS + 1):
+        for j in range(i, ITERS + 1):
+            if i + j < 2 * ITERS:
+                gram[i, j] = gram[j, i] = sum(moment[k] for k in range(j - i, i + j + 1, 2))
 
     def inner(a, b):
         total = None

time: 31.1 us -> 28.5 us (0.916)
  Pallas kernels: 30.3 us -> 27.7 us
    pallas_call x1, Pallas kernels: 29.5 us -> 26.8 us  [local(): pl.pallas_call(lambda *refs: kernel(lats, lons, *refs), out_shape=(pltpu....]
where the time goes in v3:
time: 28.5 us; the launch traced here: 28.3 us
  Pallas kernels  27.7 us (97%)
  between operations  0.64 us (2%)
    pallas_call x1, Pallas kernels, local(): pl.pallas_call(lambda *refs: kernel(lats, lons, *refs), out_shape=(pltpu....  26.8 us
    pallas_call x1, Pallas kernels, local(): pl.pallas_call(combine, out_shape=(jax.ShapeDtypeStruct((rows, cols), f32...  0.85 us

profile of v3, /device:TPU:0, one launch (start us, length us, event | category | flops | bytes accessed | tf_op | source)
XLA Modules:
  0.0 28.3 jit_solution(5224310900146975225)
XLA Ops:
  0.6 26.8 %cg.1 = (f32[128,256]{1,0:T(8,128)S(1)}, f32[128,256]{1,0:T(8,128)S(1)}, f32[128,256]{1,0:T(8,128)S(1)}, f32[128,256]{1,0:T(8,128)S(1)}, f32[128,256]{1,0:T(8,128)S(1)}, /*index=5*/f32[8,128]{1,0:T(8,128)S(1)}) custom-call(f32[128,256]{1,0:T(8,128)} %refs_0_.1, f32[128,256]{1,0:T(8,128)} %refs_1_.1, f32[128,256]{1,0:T(8,128)} %refs_2_.1, ...), custom_call_target="tpu_custom_call" | custom-call | tf_op jit(solution)/shard_map/cg/pallas_call | solution.py:377
  27.5 0.8 %combine.1 = (f32[128,256]{1,0:T(8,128)}, f32[128,256]{1,0:T(8,128)}) custom-call(f32[128,256]{1,0:T(8,128)S(1)} %get-tuple-element.8.v0_ref, f32[128,256]{1,0:T(8,128)S(1)} %get-tuple-element.9.v1_ref, f32[128,256]{1,0:T(8,128)S(1)} %get-tuple-element.10.v2_ref, f32[128,256]{1,0:T(8,128)S(1)} %get-tuple-element.11.v3_ref, ...), custom_call_target="tpu_custom_call" | custom-call | tf_op jit(solution)/shard_map/combine/pallas_call | solution.py:401

commit v4 on v3

--- a/solution.py
+++ b/solution.py
@@ -16,11 +16,10 @@
            rhs, diag, east, north, land, partner, load_sem,
            held, cols_out, rows_in, cols_in, coef_cols, coef_rows, coef_cols_in,
            send_sem, recv_sem, coef_send, coef_recv,
-           part_out, part_in, part_send, part_recv):
+           part_out, part_in, part_send, part_recv, all_in,
+           guess_out, row_in, column_in, guess_send, guess_recv):
     rows, cols = rhs.shape
-    count = lats * lons
     lat, lon = lax.axis_index("lat"), lax.axis_index("lon")
-    me = lat * lons + lon
     on_top, on_bottom = lat == lats - 1, lat == 0
 
     loads = [
@@ -34,15 +33,20 @@
 
     barrier = pltpu.get_barrier_semaphore()
 
-    def device(shift):
-        other = lax.rem(me + shift, count)
-        return (other // lons, lax.rem(other, lons))
-
-    def greet(shift, carry):
-        pl.semaphore_signal(barrier, inc=1, device_id=device(shift), device_id_type=MESH)
+    def greet_lat(step, carry):
+        pl.semaphore_signal(barrier, inc=1, device_id=(lax.rem(lat + step, lats), lon), device_id_type=MESH)
         return carry
 
-    lax.fori_loop(1, count, greet, 0)
+    def greet_lon(step, carry):
+        pl.semaphore_signal(barrier, inc=1, device_id=(lat, lax.rem(lon + step, lons)), device_id_type=MESH)
+        return carry
+
+    def pass_on(step, carry):
+        pl.semaphore_signal(all_in, inc=1, device_id=(lat, lax.rem(lon + step, lons)), device_id_type=MESH)
+        return carry
+
+    lax.fori_loop(1, lons, greet_lon, 0)
+    lax.fori_loop(1, lats, greet_lat, 0)
 
     east_id = (lat, lax.rem(lon + 1, lons))
     west_id = (lat, lax.rem(lon + lons - 1, lons))
@@ -93,7 +97,7 @@
     for coef, other in zip((east_c, west_raw, north_c, south_raw), rolled(masked)):
         guess = guess + ocean * (coef * (masked - other))
     guessed = pack((dot(v0, v0), dot(v0, guess), dot(guess, guess)))
-    part_out[0] = guessed
+    guess_out[0] = guessed
 
     own = lax.rem(partner[...], cols)
     lower = jnp.broadcast_to(lax.rem(own, 128), (8, cols))
@@ -117,7 +121,7 @@
             rows_in[k, SOUTH] = jnp.zeros((8, cols), f32)
         coef_rows[1] = jnp.zeros((8, cols), f32)
 
-    pl.semaphore_wait(barrier, count - 1)
+    pl.semaphore_wait(barrier, lats + lons - 2)
 
     def remote(src, dst, send, recv, to):
         return pltpu.make_async_remote_copy(
@@ -190,24 +194,44 @@
         def _():
             to_south.wait_send()
 
-    def part_copy(which, shift):
-        return remote(part_out.at[which], part_in.at[which, shift - 1],
-                      part_send.at[which], part_recv.at[which], device(shift))
-
-    def share(which):
-        def send(shift, carry):
-            part_copy(which, shift).start()
-            return carry
-
-        lax.fori_loop(1, count, send, 0)
-
-    def gathered(which):
-        whole = part_in.at[which]
-        pltpu.make_async_copy(whole, whole, part_recv.at[which]).wait()
-        return jnp.sum(part_in[which], axis=0)
+    def lon_at(step):
+        return (lat, lax.rem(lon + step, lons))
+
+    def lat_at(step):
+        return (lax.rem(lat + step, lats), lon)
+
+    def row_copy(step):
+        return remote(guess_out.at[0], row_in.at[step - 1], guess_send.at[0], guess_recv.at[0], lon_at(step))
+
+    def column_copy(step):
+        return remote(guess_out.at[1], column_in.at[step - 1], guess_send.at[1], guess_recv.at[1], lat_at(step))
+
+    def part_copy(up, right):
+        to = (lax.rem(lat + up, lats), lax.rem(lon + right, lons))
+        return remote(part_out, part_in.at[up * lons + right - 1], part_send.at[0], part_recv.at[0], to)
+
+    def start_row(step, carry):
+        row_copy(step).start()
+        return carry
+
+    def start_column(step, carry):
+        column_copy(step).start()
+        return carry
+
+    def await_all(whole, sem):
+        pltpu.make_async_copy(whole, whole, sem).wait()
+
+    def share():
+        for up in reversed(range(lats)):
+            def send(right, carry):
+                part_copy(up, right).start()
+                return carry
+
+            lax.fori_loop(0 if up else 1, lons, send, 0)
 
     send_halo(0)
-    share(0)
+    lax.fori_loop(1, lons, start_row, 0)
+    lax.fori_loop(1, lons, pass_on, 0)
     take_halo(0)
     coef_east.wait_recv()
 
@@ -260,23 +284,28 @@
     image = with_edges(0, interior(0, v0))
     held[1] = ocean * image
     send_halo(1)
-    packed = guessed + gathered(0)
+    await_all(row_in, guess_recv.at[0])
+    guessed = guessed + jnp.sum(row_in[...], axis=0)
+    guess_out[1] = guessed
+    lax.fori_loop(1, lats, start_column, 0)
+    plain = interior(1, image)
+    take_halo(1)
+    second = with_edges(1, plain)
+    await_all(column_in, guess_recv.at[1])
+    packed = guessed + jnp.sum(column_in[...], axis=0)
     norm = pick(packed, 0)
     shift = pick(packed, 1) / norm
     spread = pick(packed, 2) / norm - shift * shift
     sigma = jnp.sqrt(jnp.maximum(spread, 1e-4 * shift * shift))
     scale = 1.0 / sigma
     v1 = (image - shift * v0) * scale
-    second = interior(1, image) - shift * image
+    v2 = ((second - shift * image) * scale - shift * v1) * scale - v0
+    held[2] = ocean * v2
+    send_halo(2)
     v0_ref[...] = v0
     v1_ref[...] = v1
-    base2 = (second * scale - shift * v1) * scale - v0
+    v2_ref[...] = v2
     early = [dot(v0, v0), dot(v0, v1)]
-    take_halo(1)
-    v2 = base2 + with_edges(1, jnp.zeros_like(v0)) * (scale * scale)
-    held[2] = ocean * v2
-    send_halo(2)
-    v2_ref[...] = v2
     base3 = (interior(2, v2) - shift * v2) * scale - v1
     early += [dot(v0, v2), dot(v2, v2)]
     take_halo(2)
@@ -287,13 +316,15 @@
     base4 = (interior(3, v3) - shift * v3) * scale - v2
     early += [dot(v0, v3), dot(v2, v3), dot(v3, v3)]
     early = pack(early)
+    pl.semaphore_wait(all_in, lons - 1)
     take_halo(3)
     v4 = base4 + with_edges(3, jnp.zeros_like(v0)) * scale
     packed = jnp.where(lane == 7, dot(v3, v4), early)
-    part_out[1] = packed
-    share(1)
+    part_out[...] = packed
+    share()
     v4_ref[...] = v4
-    packed = packed + gathered(1)
+    await_all(part_in, part_recv.at[0])
+    packed = packed + jnp.sum(part_in[...], axis=0)
 
     p00, p01, p02, p22, p03, p23, p33, p34 = [pick(packed, k) for k in range(8)]
     moment = [p00, p01, p02, p03, p22 - p00 - p02, p23 - p01 - p03]
@@ -352,9 +383,9 @@
         end_halo(k)
     coef_east.wait_send()
     coef_fold.wait_send()
-    for which in range(2):
-        whole = part_in.at[which]
-        pltpu.make_async_copy(whole, whole, part_send.at[which]).wait()
+    await_all(row_in, guess_send.at[0])
+    await_all(column_in, guess_send.at[1])
+    await_all(part_in, part_send.at[0])
 
 
 def combine(v0_ref, v1_ref, v2_ref, v3_ref, v4_ref, mix_ref, sol_ref, res_ref):
@@ -390,8 +421,12 @@
                 pltpu.VMEM((2, 8, cols), f32),
                 pltpu.VMEM((8, rows), f32),
                 dma((ITERS, 4)), dma((ITERS, 4)), dma((2,)), dma((3,)),
+                pltpu.VMEM((1, 128), f32),
+                pltpu.VMEM((count - 1, 1, 128), f32),
+                dma((1,)), dma((1,)), pltpu.SemaphoreType.REGULAR,
                 pltpu.VMEM((2, 1, 128), f32),
-                pltpu.VMEM((2, count - 1, 1, 128), f32),
+                pltpu.VMEM((lons - 1, 1, 128), f32),
+                pltpu.VMEM((lats - 1, 1, 128), f32),
                 dma((2,)), dma((2,)),
             ],
             compiler_params=pltpu.CompilerParams(collective_id=0, has_side_effects=True),

time: 28.5 us -> 27.8 us (0.975)
  Pallas kernels: 27.7 us -> 27 us
    pallas_call x1, Pallas kernels: 26.8 us -> 26.2 us  [local(): pl.pallas_call(lambda *refs: kernel(lats, lons, *refs), out_shape=(pltpu....]
where the time goes in v4:
time: 27.8 us; the launch traced here: 27.7 us
  Pallas kernels  27 us (97%)
  between operations  0.64 us (2%)
    pallas_call x1, Pallas kernels, local(): pl.pallas_call(lambda *refs: kernel(lats, lons, *refs), out_shape=(pltpu....  26.2 us
    pallas_call x1, Pallas kernels, local(): pl.pallas_call(combine, out_shape=(jax.ShapeDtypeStruct((rows, cols), f32...  0.85 us

profile of v4, /device:TPU:0, one launch (start us, length us, event | category | flops | bytes accessed | tf_op | source)
XLA Modules:
  0.0 27.7 jit_solution(14204468759399141871)
XLA Ops:
  0.6 26.2 %cg.1 = (f32[128,256]{1,0:T(8,128)S(1)}, f32[128,256]{1,0:T(8,128)S(1)}, f32[128,256]{1,0:T(8,128)S(1)}, f32[128,256]{1,0:T(8,128)S(1)}, f32[128,256]{1,0:T(8,128)S(1)}, /*index=5*/f32[8,128]{1,0:T(8,128)S(1)}) custom-call(f32[128,256]{1,0:T(8,128)} %refs_0_.1, f32[128,256]{1,0:T(8,128)} %refs_1_.1, f32[128,256]{1,0:T(8,128)} %refs_2_.1, ...), custom_call_target="tpu_custom_call" | custom-call | tf_op jit(solution)/shard_map/cg/pallas_call | solution.py:408
  26.8 0.8 %combine.1 = (f32[128,256]{1,0:T(8,128)}, f32[128,256]{1,0:T(8,128)}) custom-call(f32[128,256]{1,0:T(8,128)S(1)} %get-tuple-element.8.v0_ref, f32[128,256]{1,0:T(8,128)S(1)} %get-tuple-element.9.v1_ref, f32[128,256]{1,0:T(8,128)S(1)} %get-tuple-element.10.v2_ref, f32[128,256]{1,0:T(8,128)S(1)} %get-tuple-element.11.v3_ref, ...), custom_call_target="tpu_custom_call" | custom-call | tf_op jit(solution)/shard_map/combine/pallas_call | solution.py:436

commit v5 on v4

--- a/solution.py
+++ b/solution.py
@@ -66,7 +66,7 @@
     def upright(row):
         return jnp.sum(jnp.where(eye, row, 0.0), axis=1, keepdims=True)
 
-    for load in loads:
+    for load in loads[:-1]:
         load.wait()
     ocean = land[...].astype(f32)
     east_c = east[...]
@@ -93,12 +93,6 @@
         return packed
 
     west_raw, south_raw = pltpu.roll(east_c, 1, 1), pltpu.roll(north_c, 1, 0)
-    guess = diag[...] * v0
-    for coef, other in zip((east_c, west_raw, north_c, south_raw), rolled(masked)):
-        guess = guess + ocean * (coef * (masked - other))
-    guessed = pack((dot(v0, v0), dot(v0, guess), dot(guess, guess)))
-    guess_out[0] = guessed
-
     own = lax.rem(partner[...], cols)
     lower = jnp.broadcast_to(lax.rem(own, 128), (8, cols))
     panel = jnp.broadcast_to(own // 128, (8, cols))
@@ -121,6 +115,11 @@
             rows_in[k, SOUTH] = jnp.zeros((8, cols), f32)
         coef_rows[1] = jnp.zeros((8, cols), f32)
 
+    def strip_columns(k, field):
+        cols_out[k, 0] = jnp.broadcast_to(flat(field[:, cols - 1:]), (8, rows))
+        cols_out[k, 1] = jnp.broadcast_to(flat(field[:, :1]), (8, rows))
+
+    strip_columns(0, masked)
     pl.semaphore_wait(barrier, lats + lons - 2)
 
     def remote(src, dst, send, recv, to):
@@ -168,9 +167,8 @@
         def _():
             to_south.start()
 
-        masked = held[k]
-        cols_out[k, 0] = jnp.broadcast_to(flat(masked[:, cols - 1:]), (8, rows))
-        cols_out[k, 1] = jnp.broadcast_to(flat(masked[:, :1]), (8, rows))
+        if k:
+            strip_columns(k, held[k])
         to_east.start()
         to_west.start()
 
@@ -230,6 +228,12 @@
             lax.fori_loop(0 if up else 1, lons, send, 0)
 
     send_halo(0)
+    loads[-1].wait()
+    guess = diag[...] * v0
+    for coef, other in zip((east_c, west_raw, north_c, south_raw), rolled(masked)):
+        guess = guess + ocean * (coef * (masked - other))
+    guessed = pack((dot(v0, v0), dot(v0, guess), dot(guess, guess)))
+    guess_out[0] = guessed
     lax.fori_loop(1, lons, start_row, 0)
     lax.fori_loop(1, lons, pass_on, 0)
     take_halo(0)

time: 27.8 us -> 27.7 us (level)
  no operation moved by 1% of the time
where the time goes in v5:
time: 27.7 us; the launch traced here: 27.6 us
  Pallas kernels  26.9 us (97%)
  between operations  0.64 us (2%)
    pallas_call x1, Pallas kernels, local(): pl.pallas_call(lambda *refs: kernel(lats, lons, *refs), out_shape=(pltpu....  26.1 us
    pallas_call x1, Pallas kernels, local(): pl.pallas_call(combine, out_shape=(jax.ShapeDtypeStruct((rows, cols), f32...  0.85 us

profile of v5, /device:TPU:0, one launch (start us, length us, event | category | flops | bytes accessed | tf_op | source)
XLA Modules:
  0.0 27.6 jit_solution(775550994540645981)
XLA Ops:
  0.6 26.1 %cg.1 = (f32[128,256]{1,0:T(8,128)S(1)}, f32[128,256]{1,0:T(8,128)S(1)}, f32[128,256]{1,0:T(8,128)S(1)}, f32[128,256]{1,0:T(8,128)S(1)}, f32[128,256]{1,0:T(8,128)S(1)}, /*index=5*/f32[8,128]{1,0:T(8,128)S(1)}) custom-call(f32[128,256]{1,0:T(8,128)} %refs_0_.1, f32[128,256]{1,0:T(8,128)} %refs_1_.1, f32[128,256]{1,0:T(8,128)} %refs_2_.1, ...), custom_call_target="tpu_custom_call" | custom-call | tf_op jit(solution)/shard_map/cg/pallas_call | solution.py:412
  26.7 0.8 %combine.1 = (f32[128,256]{1,0:T(8,128)}, f32[128,256]{1,0:T(8,128)}) custom-call(f32[128,256]{1,0:T(8,128)S(1)} %get-tuple-element.8.v0_ref, f32[128,256]{1,0:T(8,128)S(1)} %get-tuple-element.9.v1_ref, f32[128,256]{1,0:T(8,128)S(1)} %get-tuple-element.10.v2_ref, f32[128,256]{1,0:T(8,128)S(1)} %get-tuple-element.11.v3_ref, ...), custom_call_target="tpu_custom_call" | custom-call | tf_op jit(solution)/shard_map/combine/pallas_call | solution.py:440

commit v6 on v5

--- a/solution.py
+++ b/solution.py
@@ -340,39 +340,35 @@
             if i + j < 2 * ITERS:
                 gram[i, j] = gram[j, i] = sum(moment[k] for k in range(j - i, i + j + 1, 2))
 
-    def inner(a, b):
-        total = None
-        for i, x in enumerate(a):
-            line = None
-            for j, y in enumerate(b):
-                term = gram[i, j] * y
-                line = term if line is None else line + term
-            total = x * line if total is None else total + x * line
-        return total
-
-    def image_of(a):
-        out = []
-        for k in range(len(a) + 1):
-            term = shift * a[k] if k < len(a) else None
-            for near in (k - 1, k + 1):
-                if 0 <= near < len(a):
-                    term = sigma * a[near] if term is None else term + sigma * a[near]
-            out.append(term)
-        return out
-
-    one = jnp.ones((1, 1), f32)
-    left, way, found = [one], [one], []
-    rr = inner(left, left)
-    for step in range(ITERS):
-        along = image_of(way)
-        alpha = rr / inner(way, along)
-        found = [(found[k] + alpha * w) if k < len(found) else alpha * w for k, w in enumerate(way)]
-        left = [(left[k] - alpha * a) if k < len(left) else -alpha * a for k, a in enumerate(along)]
-        if step + 1 < ITERS:
-            new = inner(left, left)
-            ratio = new / rr
-            way = [(left[k] + ratio * way[k]) if k < len(way) else left[k] for k in range(len(left))]
-            rr = new
+    def energy(i, j):
+        total = shift * gram[i, j] + sigma * gram[i, j + 1]
+        return total + sigma * gram[i, j - 1] if j else total
+
+    system = {(i, j): energy(i, j) for i in range(ITERS) for j in range(i, ITERS)}
+    goal = [gram[0, i] for i in range(ITERS)]
+    inverse = []
+    for k in range(ITERS):
+        inverse.append(1.0 / system[k, k])
+        for i in range(k + 1, ITERS):
+            factor = system[k, i] * inverse[k]
+            goal[i] = goal[i] - factor * goal[k]
+            for j in range(i, ITERS):
+                system[i, j] = system[i, j] - factor * system[k, j]
+    found = [None] * ITERS
+    for k in reversed(range(ITERS)):
+        value = goal[k]
+        for j in range(k + 1, ITERS):
+            value = value - system[k, j] * found[j]
+        found[k] = value * inverse[k]
+    left = []
+    for k in range(ITERS + 1):
+        value = jnp.full((1, 1), 0.0 if k else 1.0, f32)
+        if k < ITERS:
+            value = value - shift * found[k]
+        for near in (k - 1, k + 1):
+            if 0 <= near < ITERS:
+                value = value - sigma * found[near]
+        left.append(value)
 
     weights = jnp.zeros((8, 128), f32)
     spot = 128 * lax.broadcasted_iota(jnp.int32, (8, 128), 0) + lax.broadcasted_iota(

time: 27.7 us -> 26.9 us (0.971)
  Pallas kernels: 26.9 us -> 26.1 us
    pallas_call x1, Pallas kernels: 26.1 us -> 25.3 us  [local(): pl.pallas_call(lambda *refs: kernel(lats, lons, *refs), out_shape=(pltpu....]
where the time goes in v6:
time: 26.9 us; the launch traced here: 26.7 us
  Pallas kernels  26.1 us (97%)
  between operations  0.64 us (2%)
    pallas_call x1, Pallas kernels, local(): pl.pallas_call(lambda *refs: kernel(lats, lons, *refs), out_shape=(pltpu....  25.3 us
    pallas_call x1, Pallas kernels, local(): pl.pallas_call(combine, out_shape=(jax.ShapeDtypeStruct((rows, cols), f32...  0.85 us

profile of v6, /device:TPU:0, one launch (start us, length us, event | category | flops | bytes accessed | tf_op | source)
XLA Modules:
  0.0 26.7 jit_solution(15600338422025620649)
XLA Ops:
  0.6 25.3 %cg.1 = (f32[128,256]{1,0:T(8,128)S(1)}, f32[128,256]{1,0:T(8,128)S(1)}, f32[128,256]{1,0:T(8,128)S(1)}, f32[128,256]{1,0:T(8,128)S(1)}, f32[128,256]{1,0:T(8,128)S(1)}, /*index=5*/f32[8,128]{1,0:T(8,128)S(1)}) custom-call(f32[128,256]{1,0:T(8,128)} %refs_0_.1, f32[128,256]{1,0:T(8,128)} %refs_1_.1, f32[128,256]{1,0:T(8,128)} %refs_2_.1, ...), custom_call_target="tpu_custom_call" | custom-call | tf_op jit(solution)/shard_map/cg/pallas_call | solution.py:408
  25.9 0.8 %combine.1 = (f32[128,256]{1,0:T(8,128)}, f32[128,256]{1,0:T(8,128)}) custom-call(f32[128,256]{1,0:T(8,128)S(1)} %get-tuple-element.8.v0_ref, f32[128,256]{1,0:T(8,128)S(1)} %get-tuple-element.9.v1_ref, f32[128,256]{1,0:T(8,128)S(1)} %get-tuple-element.10.v2_ref, f32[128,256]{1,0:T(8,128)S(1)} %get-tuple-element.11.v3_ref, ...), custom_call_target="tpu_custom_call" | custom-call | tf_op jit(solution)/shard_map/combine/pallas_call | solution.py:436
